TPU v7x, 256 devices: a whole 4x4x8 slice. The times are simulated.
256 devices in a mesh: req: 128 (over x, y, z), head: 2 (over core).
Axes of the slice: x: 4, y: 4, z: 8, core: 2. Of those that a mesh axis runs over, the one named last changes fastest.
Arguments:
- verify_x: bfloat16 [128, 5, 2048], P('req'), may hold values from -6 to 6
- prefill_x: bfloat16 [32768, 2048], P('req'), may hold values from -6 to 6
- attn_gain: float32 [2048], replicated, may hold values from 0.25 to 1.75
- w_query: bfloat16 [2048, 2048], P(None, 'head'), may hold values from -0.125 to 0.125
- w_keyval: bfloat16 [2048, 1024], P(None, 'head'), may hold values from -0.125 to 0.125
- qk_gain: float32 [2, 256], replicated, may hold values from 0.25 to 8
- w_out: bfloat16 [2048, 2048], P('head'), may hold values from -0.125 to 0.125
- post_gain: float32 [2048], replicated, may hold values from 0.1 to 1.9
- page_pool: bfloat16 [8192, 16, 1024], P('req', None, 'head'), may hold values from -6 to 6
- outbound: int32 [128, 128], P('req'), may hold values from -1 to 63, as said below
- page_table: int32 [128, 64], P('req'), may hold values from 0 to 191, as said below
- cache_len: int32 [128], P('req'), may hold values from 1 to 1024, as said below
- prompt_len: int32 [128, 4], P('req'), may hold values from 1 to 128, 256 in all within a row
- accepted: int32 [128], P('req'), may hold values from 0 to 5
Outputs:
- verify_out: bfloat16 [128, 5, 2048], P('req', None, 'head')
- prefill_out: bfloat16 [32768, 2048], P('req', 'head')
- verify_kv: bfloat16 [128, 5, 1024], P('req', None, 'head')
- prefill_kv: bfloat16 [32768, 1024], P('req', 'head')
Inputs may be any that keep to these rules, and one draw needn't show every extreme that they name: `outbound`: row s names a page of device s's pool for every device d other than s; the entry at d = s is -1. `page_table`: an entry below 64 names a page of the device's own pool; an entry 64 + s names the page received from device s, s never the device itself. `cache_len`: some request has exactly 1024 cached tokens.
All inputs are finite; a program needn't handle non-finite values.
Results may differ from a plain program's by a relative error of at most 0.015.
The roundings to bfloat16 on the way count: a program that leaves them out, or rounds other values in their place, can miss the bound.
Values may be sent and summed in bfloat16 or wider, within the bound.
No kernel may reach another device: no remote copies, remote signals or barrier semaphores. Data moves between devices by JAX's collectives and lax.ppermute only.
A program may use at most 64 MiB of HBM per device.

v0:
```python
import jax
import jax.numpy as jnp
from jax import lax
from jax.sharding import PartitionSpec as P

HEAD = 256
eps_norm = 1e-06
rope_base = 1000000.0
neg_large = -1e30


def rms_scale(values):
    return values * lax.rsqrt(jnp.mean(values * values, axis=-1, keepdims=True) + eps_norm)


def rotate(values, position):
    half_dim = values.shape[-1] // 2
    inv_freq = rope_base ** (-(jnp.arange(half_dim, dtype=jnp.float32) * 2.0) / values.shape[-1])
    angles = position[:, None, None] * inv_freq[None, None, :]
    cosine = jnp.cos(angles)
    sine_part = jnp.sin(angles)
    first = values[..., :half_dim]
    second = values[..., half_dim:]
    return jnp.concatenate(
        [first * cosine - second * sine_part, second * cosine + first * sine_part], axis=-1
    )


def project(hidden_rows, attn_gain, w_query, w_keyval, qk_gain, position):
    row_count = hidden_rows.shape[0]
    normed = (rms_scale(hidden_rows.astype(jnp.float32)) * attn_gain).astype(jnp.bfloat16)
    query_rows = jnp.dot(normed, w_query, preferred_element_type=jnp.float32).reshape(
        row_count, -1, HEAD
    )
    query_rows = rotate(rms_scale(query_rows) * qk_gain[0], position).astype(jnp.bfloat16)
    keyval = jnp.dot(normed, w_keyval, preferred_element_type=jnp.float32).reshape(
        row_count, -1, 2, HEAD
    )
    key_rows = rotate(rms_scale(keyval[:, :, 0]) * qk_gain[1], position).astype(jnp.bfloat16)
    value_rows = rms_scale(keyval[:, :, 1]).astype(jnp.bfloat16)
    return (query_rows, key_rows, value_rows)


def attend(query_rows, key_rows, value_rows, allowed):
    row_count = query_rows.shape[0]
    groups = key_rows.shape[1]
    grouped = query_rows.reshape(row_count, groups, -1, HEAD)
    scores = jnp.einsum("tgqe,jge->gqtj", grouped, key_rows, preferred_element_type=jnp.float32)
    scores = jnp.where(allowed[None, None], scores, neg_large)
    peak_score = jnp.max(scores, axis=-1, keepdims=True)
    weights = jnp.exp(scores - peak_score)
    denom_sum = jnp.sum(weights, axis=-1, keepdims=True)
    attn_probs = (weights / denom_sum).astype(jnp.bfloat16)
    mixed_heads = jnp.einsum(
        "gqtj,jge->tgqe", attn_probs, value_rows, preferred_element_type=jnp.float32
    )
    return mixed_heads.reshape(row_count, -1).astype(jnp.bfloat16)


def prompt_layout(lengths, row_count):
    prompt_ends = jnp.cumsum(lengths)
    row_index = jnp.arange(row_count, dtype=jnp.int32)
    segment = jnp.sum((row_index[:, None] >= prompt_ends[None, :]).astype(jnp.int32), axis=1)
    starts = prompt_ends - lengths
    which = segment[:, None] == jnp.arange(lengths.shape[0], dtype=jnp.int32)[None, :]
    start_row = jnp.sum(jnp.where(which, starts[None, :], 0), axis=1)
    position = (row_index - start_row).astype(jnp.float32)
    allowed = (segment[:, None] == segment[None, :]) & (row_index[None, :] <= row_index[:, None])
    return (position, allowed)


def on_device(
    verify_x,
    prefill_x,
    attn_gain,
    w_query,
    w_keyval,
    qk_gain,
    w_out,
    post_gain,
    page_pool,
    outbound,
    page_table,
    cache_len,
    prompt_len,
    accepted,
):
    req_count, draft_len, width = verify_x.shape
    pref_rows = prefill_x.shape[0]
    sent_page = outbound[0]
    outgoing = jnp.take(page_pool, jnp.clip(sent_page, 0, page_pool.shape[0] - 1), axis=0)
    outgoing = jnp.where((sent_page >= 0)[:, None, None], outgoing, jnp.zeros_like(outgoing))
    arrived = lax.all_to_all(outgoing, "req", split_axis=0, concat_axis=0, tiled=True)
    pool_now = jnp.concatenate([page_pool, arrived], axis=0)
    verify_pos = (
        (cache_len[:, None] + jnp.arange(draft_len, dtype=jnp.int32)[None, :])
        .astype(jnp.float32)
        .reshape(-1)
    )
    prefill_pos, prefill_allowed = prompt_layout(prompt_len[0], pref_rows)
    all_rows = jnp.concatenate([verify_x.reshape(-1, width), prefill_x], axis=0)
    position = jnp.concatenate([verify_pos, prefill_pos], axis=0)
    query_rows, key_rows, value_rows = project(
        all_rows, attn_gain, w_query, w_keyval, qk_gain, position
    )
    groups = key_rows.shape[1]
    verify_count = req_count * draft_len

    def verify_one(query_part, key_part, value_part, page_list, length):
        cached = jnp.take(pool_now, page_list, axis=0).reshape(-1, groups, 2, HEAD)
        cache_rows = cached.shape[0]
        all_keys = jnp.concatenate([cached[:, :, 0], key_part], axis=0)
        all_values = jnp.concatenate([cached[:, :, 1], value_part], axis=0)
        slot = jnp.arange(cache_rows + draft_len, dtype=jnp.int32)
        step_index = jnp.arange(draft_len, dtype=jnp.int32)
        allowed = jnp.where(
            slot[None, :] < cache_rows,
            slot[None, :] < length,
            slot[None, :] - cache_rows <= step_index[:, None],
        )
        return attend(query_part, all_keys, all_values, allowed)

    verify_attn = jax.vmap(verify_one)(
        query_rows[:verify_count].reshape(req_count, draft_len, -1, HEAD),
        key_rows[:verify_count].reshape(req_count, draft_len, groups, HEAD),
        value_rows[:verify_count].reshape(req_count, draft_len, groups, HEAD),
        page_table,
        cache_len,
    )
    prefill_attn = attend(
        query_rows[verify_count:],
        key_rows[verify_count:],
        value_rows[verify_count:],
        prefill_allowed,
    )
    all_attn = jnp.concatenate([verify_attn.reshape(verify_count, -1), prefill_attn], axis=0)
    partial_rows = jnp.dot(all_attn, w_out, preferred_element_type=jnp.float32)
    half_cols = width // lax.axis_size("head")
    offset = lax.axis_index("head") * half_cols
    summed = lax.psum(partial_rows, "head")
    own_part = lax.dynamic_slice_in_dim(rms_scale(summed), offset, half_cols, 1)
    residual = lax.dynamic_slice_in_dim(all_rows, offset, half_cols, 1).astype(jnp.float32)
    gain_part = lax.dynamic_slice_in_dim(post_gain, offset, half_cols, 0)
    final = (residual + own_part * gain_part).astype(jnp.bfloat16)
    verify_out = final[:verify_count].reshape(req_count, draft_len, half_cols)
    prefill_out = final[verify_count:]
    new_cache = jnp.stack([key_rows, value_rows], axis=2).reshape(all_rows.shape[0], -1)
    verify_cache = new_cache[:verify_count].reshape(req_count, draft_len, -1)
    keep_rows = jnp.arange(draft_len, dtype=jnp.int32)[None, :, None] < accepted[:, None, None]
    verify_kv = jnp.where(keep_rows, verify_cache, jnp.zeros_like(verify_cache))
    prefill_kv = new_cache[verify_count:]
    return (verify_out, prefill_out, verify_kv, prefill_kv)


def solution(mesh):
    placed = (
        P("req", None, None),
        P("req", None),
        P(),
        P(None, "head"),
        P(None, "head"),
        P(),
        P("head", None),
        P(),
        P("req", None, "head"),
        P("req", None),
        P("req", None),
        P("req"),
        P("req", None),
        P("req"),
    )
    return jax.shard_map(
        on_device,
        mesh=mesh,
        in_specs=placed,
        out_specs=(
            P("req", None, "head"),
            P("req", "head"),
            P("req", None, "head"),
            P("req", "head"),
        ),
        check_vma=False,
    )
```

profile of v0, /device:TPU:1, one launch (start us, length us, event | category | flops | bytes accessed | tf_op | source)
XLA Modules:
  0.0 138.2 jit_solution(2135943802772641248)
XLA Ops:
  9.3 3.3 %gather_fusion = bf16[128,16,512]{2,1,0:T(8,128)(2,1)} fusion(bf16[64,16,512]{2,1,0:T(8,128)(2,1)} %param.22, s32[1024]{0:T(1024)S(1)} %pad_clamp_fusion.1), kind=kCustom, calls=%fused_computation | custom fusion | bytes 4194816 | tf_op jit(solution)/shard_map/jit(_take)/gather | solution.py:91
  12.6 3.0 %select_select_fusion = bf16[128,16,512]{2,1,0:T(8,128)(2,1)} fusion(bf16[128,16,512]{2,1,0:T(8,128)(2,1)} %gather_fusion, pred[128]{0:T(512)(128)(4,1)S(1)} %compare_and_fusion, pred[128]{0:T(512)(128)(4,1)S(1)} %compare_bitcast_fusion), kind=kLoop, calls=%fused_computation.11 | loop fusion | flops 2097152 | bytes 4194560 | tf_op jit(solution)/shard_map/jit(_where)/select_n | solution.py:92
  15.6 17.0 %all-to-all-start = ((bf16[128,16,512]{2,1,0:T(8,128)(2,1)}), bf16[128,16,512]{2,1,0:T(8,128)(2,1)}, u32[]{:S(2)}, u32[]{:S(2)}) async-start(bf16[128,16,512]{2,1,0:T(8,128)(2,1)} %select_select_fusion), calls=%async_computation | async-start | bytes 4194304 | tf_op jit(solution)/shard_map/all_to_all | solution.py:93
  34.0 1.6 %fusion.51 = f32[261,512]{1,0:T(8,128)} fusion(bf16[2048,512]{1,0:T(8,128)(2,1)S(1)} %copy-done, f32[2048]{0:T(1024)S(1)} %copy-done.17, f32[261]{0:T(512)S(1)} %add_rsqrt_fusion.4, bf16[256,2048]{1,0:T(8,128)(2,1)S(1)} %copy-done.3, bf16[5,2048]{1,0:T(8,128)(2,1)S(1)} %bitcast.115), kind=kOutput, calls=%fused_computation.125 | convolution fusion | flops 551098368 | bytes 3709972 | tf_op jit(solution)/shard_map/dot_general | solution.py:36
  35.6 2.2 %reshape.682 = f32[261,1,2,256]{3,2,0,1:T(2,128)} reshape(f32[261,512]{1,0:T(8,128)} %fusion.51) | data formatting | bytes 1069056 | tf_op jit(solution)/shard_map/reshape | solution.py:36
  37.8 1.7 %fusion.53 = (f32[261,1,1,256]{3,2,0,1:T(1,128)S(1)}, f32[261,1,1,256]{3,2,0,1:T(1,128)S(1)}) fusion(f32[261,1,2,256]{3,2,0,1:T(2,128)} %reshape.682), kind=kLoop, calls=%fused_computation.126 | loop fusion | bytes 1069056 | tf_op jit(solution)/shard_map/slice | solution.py:40
  41.3 4.6 %fusion.49 = f32[261,1024]{1,0:T(8,128)} fusion(bf16[2048,1024]{1,0:T(8,128)(2,1)} %param.17, f32[2048]{0:T(1024)S(1)} %copy-done.17, f32[261]{0:T(512)S(1)} %add_rsqrt_fusion.4, bf16[256,2048]{1,0:T(8,128)(2,1)S(1)} %copy-done.3, bf16[5,2048]{1,0:T(8,128)(2,1)S(1)} %bitcast.116), kind=kOutput, calls=%fused_computation.124 | convolution fusion | flops 1098455040 | bytes 6341652 | tf_op jit(solution)/shard_map/dot_general | solution.py:32
  45.9 1.8 %reshape.689 = f32[261,4,256]{2,1,0:T(4,128)S(1)} reshape(f32[261,1024]{1,0:T(8,128)} %fusion.49) | data formatting | bytes 2138112 | tf_op jit(solution)/shard_map/reshape | solution.py:32
  47.7 1.0 multiply_reduce_fusion.1
  48.7 1.0 copy.55
  51.8 1.1 fusion.21
  52.9 1.3 fusion.29
  54.3 1.2 multiply_cosine_fusion
  56.7 1.2 convolution_convert_fusion
  57.9 27.0 %all-to-all-done = bf16[128,16,512]{2,1,0:T(8,128)(2,1)} async-done(((bf16[128,16,512]{2,1,0:T(8,128)(2,1)}), bf16[128,16,512]{2,1,0:T(8,128)(2,1)}, u32[]{:S(2)}, u32[]{:S(2)}) %all-to-all-start) | async-done | bytes 2097184 | tf_op jit(solution)/shard_map/all_to_all | solution.py:93
  84.9 3.5 %pad_maximum_fusion = bf16[192,16,512]{2,1,0:T(8,128)(2,1)} fusion(bf16[128,16,512]{2,1,0:T(8,128)(2,1)} %all-to-all-done, bf16[64,16,512]{2,1,0:T(8,128)(2,1)S(1)} %copy-done.1), kind=kLoop, calls=%fused_computation.2 | loop fusion | flops 1572864 | bytes 6291456 | tf_op jit(solution)/shard_map/concatenate | solution.py:94
  88.4 2.6 %gather_fusion.1 = bf16[64,16,512]{2,1,0:T(8,128)(2,1)S(1)} fusion(bf16[192,16,512]{2,1,0:T(8,128)(2,1)} %pad_maximum_fusion, s32[1024]{0:T(1024)} %pad_clamp_fusion), kind=kCustom, calls=%fused_computation.1 | custom fusion | bytes 2097408 | tf_op jit(solution)/shard_map/vmap(jit(_take))/gather | solution.py:110
  91.1 1.1 gather.12
  92.2 1.5 %copy_select_fusion = bf16[1,1024,1,2,256]{4,1,3,2,0:T(8,128)(2,1)S(1)} fusion(bf16[1,1024,1,2,256]{4,3,1,2,0:T(2,128)(2,1)} %gather.12, pred[1024]{0:T(1024)(128)(4,1)S(1)} %copy-done.15), kind=kLoop, calls=%fused_computation.25 | loop fusion | flops 524288 | bytes 2098176 | tf_op jit(solution)/shard_map/vmap(jit(_take))/select_n | solution.py:110
  94.8 4.9 %fusion.10 = f32[261,2048]{1,0:T(8,128)} fusion(bf16[1024,2048]{1,0:T(8,128)(2,1)} %param.20, bf16[256,1024]{0,1:T(8,128)(2,1)S(1)} %bitcast.123, bf16[5,1024]{0,1:T(8,128)(2,1)S(1)} %copy.59), kind=kOutput, calls=%fused_computation.30 | convolution fusion | flops 1095782400 | bytes 6866944 | tf_op jit(solution)/shard_map/dot_general | solution.py:137
  100.5 1.7 %pad_maximum_fusion.4 = bf16[256,1,2,256]{3,0,2,1:T(8,128)(2,1)} fusion(bf16[261,1,1,256]{3,0,2,1:T(8,128)(2,1)S(1)} %multiply_convert_fusion, bf16[261,1,1,128]{3,0,2,1:T(8,128)(2,1)} %bitcast.111, bf16[261,1,1,128]{3,0,2,1:T(8,128)(2,1)S(1)} %bitcast.109), kind=kLoop, calls=%fused_computation.56 | loop fusion | flops 786432 | bytes 529408 | tf_op jit(solution)/shard_map/stack | solution.py:147
  102.2 1.1 copy.60
  106.2 20.9 %all-reduce.2.cloned.1.call-done = f32[261,2048]{1,0:T(8,128)} async-done(((f32[261,2048]{1,0:T(8,128)}), f32[261,2048]{1,0:T(8,128)}) %all-reduce.2.cloned.1.call-update) | async-done | bytes 2138128 | tf_op jit(solution)/shard_map/psum | solution.py:140
  127.1 2.0 %multiply_reduce_fusion = f32[261]{0:T(512)S(1)} fusion(f32[261,2048]{1,0:T(8,128)} %all-reduce.2.cloned.1.call-done), kind=kLoop, calls=%fused_computation.10 | loop fusion | flops 1068795 | bytes 2139156 | tf_op jit(solution)/shard_map/reduce_sum | solution.py:13
  (95 shorter events, 14.3 us)
Async XLA Ops:
  7.2 26.8 %copy-start = (bf16[2048,512]{1,0:T(8,128)(2,1)S(1)}, bf16[2048,512]{1,0:T(8,128)(2,1)}, u32[]{:S(2)}) copy-start(bf16[2048,512]{1,0:T(8,128)(2,1)} %param.18) | copy-start | bytes 6291460
  15.6 17.9 %copy-start.18 = (s32[1,64]{1,0:T(1,128)S(1)}, s32[1,64]{1,0:T(1,128)}, u32[]{:S(2)}) copy-start(s32[1,64]{1,0:T(1,128)} %param.24) | copy-start | bytes 772
  15.6 17.9 %copy-start.3 = (bf16[256,2048]{1,0:T(8,128)(2,1)S(1)}, bf16[256,2048]{1,0:T(8,128)(2,1)}, u32[]{:S(2)}) copy-start(bf16[256,2048]{1,0:T(8,128)(2,1)} %param.15) | copy-start | bytes 3145732
  15.6 17.9 %copy-start.12 = (bf16[1,5,2048]{2,1,0:T(8,128)(2,1)S(1)}, bf16[1,5,2048]{2,1,0:T(8,128)(2,1)}, u32[]{:S(2)}) copy-start(bf16[1,5,2048]{2,1,0:T(8,128)(2,1)} %param.14) | copy-start | bytes 61444
  15.6 18.4 %copy-start.17 = (f32[2048]{0:T(1024)S(1)}, f32[2048]{0:T(1024)}, u32[]{:S(2)}) copy-start(f32[2048]{0:T(1024)} %param.16) | copy-start | bytes 24580
  15.6 69.3 %all-to-all-start = ((bf16[128,16,512]{2,1,0:T(8,128)(2,1)}), bf16[128,16,512]{2,1,0:T(8,128)(2,1)}, u32[]{:S(2)}, u32[]{:S(2)}) async-start(bf16[128,16,512]{2,1,0:T(8,128)(2,1)} %select_select_fusion), calls=%async_computation | async-start | bytes 4194304 | tf_op jit(solution)/shard_map/all_to_all | solution.py:93
  32.6 94.4 %all-reduce.2.cloned.1.call-start = ((), (), s32[]{:S(2)}) async-start(), calls=%async_computation.1 | async-start | bytes 4325376 | tf_op jit(solution)/shard_map/psum | solution.py:140
  35.6 4.7 %copy-start.19 = (s32[1,4]{1,0:T(1,128)S(1)}, s32[1,4]{1,0:T(1,128)}, u32[]{:S(2)}) copy-start(s32[1,4]{1,0:T(1,128)} %param.26) | copy-start | bytes 52
  39.4 0.7 copy-start.5
  45.9 5.8 %copy-start.16 = (f32[2,256]{1,0:T(2,128)S(1)}, f32[2,256]{1,0:T(2,128)}, u32[]{:S(2)}) copy-start(f32[2,256]{1,0:T(2,128)} %param.19) | copy-start | bytes 6148
  54.2 1.8 %copy-start.7 = (bf16[261,1,128]{2,0,1:T(8,128)(2,1)}, bf16[261,1,128]{2,0,1:T(8,128)(2,1)S(1)}, u32[]{:S(2)}) copy-start(bf16[261,1,128]{2,0,1:T(8,128)(2,1)S(1)} %get-tuple-element.27) | copy-start | bytes 200452
  56.0 1.9 %copy-start.8 = (bf16[261,4,128]{2,0,1:T(8,128)(2,1)}, bf16[261,4,128]{2,0,1:T(8,128)(2,1)S(1)}, u32[]{:S(2)}) copy-start(bf16[261,4,128]{2,0,1:T(8,128)(2,1)S(1)} %get-tuple-element.20) | copy-start | bytes 801796
  56.0 1.9 %copy-start.10 = (bf16[261,4,128]{2,0,1:T(8,128)(2,1)}, bf16[261,4,128]{2,0,1:T(8,128)(2,1)S(1)}, u32[]{:S(2)}) copy-start(bf16[261,4,128]{2,0,1:T(8,128)(2,1)S(1)} %get-tuple-element.21) | copy-start | bytes 801796
  56.7 1.2 copy-start.13
  56.7 1.2 copy-start.14
  56.7 28.2 %copy-start.1 = (bf16[64,16,512]{2,1,0:T(8,128)(2,1)S(1)}, bf16[64,16,512]{2,1,0:T(8,128)(2,1)}, u32[]{:S(2)}) copy-start(bf16[64,16,512]{2,1,0:T(8,128)(2,1)} %param.22) | copy-start | bytes 3145732
  88.4 3.8 %copy-start.15 = (pred[1024]{0:T(1024)(128)(4,1)S(1)}, pred[1024]{0:T(1024)(128)(4,1)}, u32[]{:S(2)}) copy-start(pred[1024]{0:T(1024)(128)(4,1)} %broadcast_in_dim.141) | copy-start | bytes 3076
  92.2 1.6 %copy-start.9 = (bf16[261,4,128]{2,0,1:T(8,128)(2,1)S(1)}, bf16[261,4,128]{2,0,1:T(8,128)(2,1)}, u32[]{:S(2)}) copy-start(bf16[261,4,128]{2,0,1:T(8,128)(2,1)} %copy-done.8) | copy-start | bytes 801796
  92.2 1.6 %copy-start.11 = (bf16[261,4,128]{2,0,1:T(8,128)(2,1)S(1)}, bf16[261,4,128]{2,0,1:T(8,128)(2,1)}, u32[]{:S(2)}) copy-start(bf16[261,4,128]{2,0,1:T(8,128)(2,1)} %copy-done.10) | copy-start | bytes 801796
  93.8 1.0 copy-start.20
  99.9 0.7 copy-start.6
  99.9 29.2 %copy-start.4 = (bf16[256,2048]{1,0:T(8,128)(2,1)S(1)}, bf16[256,2048]{1,0:T(8,128)(2,1)}, u32[]{:S(2)}) copy-start(bf16[256,2048]{1,0:T(8,128)(2,1)} %param.15) | copy-start | bytes 3145732
  104.8 24.3 %dynamic-slice-start = ((f32[2048]{0:T(1024)}, s32[]{:T(128)}), f32[1024]{0:T(1024)S(1)}, s32[]{:S(2)}) async-start(f32[2048]{0:T(1024)} %param.21, s32[]{:T(128)} %select_n.81), calls=%async_computation.2 | async-start | bytes 8704 | tf_op jit(solution)/shard_map/dynamic_slice | solution.py:143
  127.1 2.3 %copy-start.2 = (f32[261,2048]{1,0:T(8,128)S(1)}, f32[261,2048]{1,0:T(8,128)}, u32[]{:S(2)}) copy-start(f32[261,2048]{1,0:T(8,128)} %all-reduce.2.cloned.1.call-done) | copy-start | bytes 6414340
Sparse Core Ops, SparseCore 0:
  99.9 27.1 all-reduce.1
where the time goes:
time: 139 us; the launch traced here: 138 us
  waiting for transfers between devices  47.9 us (34%)
  other arithmetic  24.3 us (17%)
  local copies, waits for them, and re-layouts  19.8 us (14%)
  starting transfers between devices  17.2 us (12%)
  between operations  15.7 us (11%)
  matrix products  13.3 us (10%)
    all_to_all x1, waiting for transfers between devices, on_device(): lax.all_to_all(outgoing, 'req', split_axis=0, concat_axis=0, tiled=True)  27 us
    psum x1, waiting for transfers between devices, on_device(): summed = lax.psum(partial_rows, 'head')  20.9 us
    all_to_all x1, starting transfers between devices, on_device(): lax.all_to_all(outgoing, 'req', split_axis=0, concat_axis=0, tiled=True)  17 us
    dot_general x1, matrix products, on_device(): partial_rows = jnp.dot(all_attn, w_out, preferred_element_type=jnp.float32)  4.91 us
    reduce_sum x5, other arithmetic, rms_scale(): jnp.mean(values * values, axis=-1, keepdims=True) + eps_norm  4.76 us
    dot_general x1, matrix products, project(): jnp.dot(normed, w_query, preferred_element_type=jnp.float32)  4.6 us
    gather x2, local copies, waits for them, and re-layouts, verify_one(): cached = jnp.take(pool_now, page_list, axis=0).reshape(-1, groups, 2, HEAD)  3.76 us
    concatenate x1, other arithmetic, on_device(): pool_now = jnp.concatenate([page_pool, arrived], axis=0)  3.53 us
  transfers between devices with their start and end apart: 2, of which 2 were waited for; matrix products, arithmetic and copies ran while one was open for 21% of the time, Pallas kernels for 0%

commit v1 on v0

--- a/solution.py
+++ b/solution.py
@@ -137,7 +137,7 @@
     partial_rows = jnp.dot(all_attn, w_out, preferred_element_type=jnp.float32)
     half_cols = width // lax.axis_size("head")
     offset = lax.axis_index("head") * half_cols
-    summed = lax.psum(partial_rows, "head")
+    summed = jnp.sum(lax.all_gather(partial_rows, "head"), axis=0)
     own_part = lax.dynamic_slice_in_dim(rms_scale(summed), offset, half_cols, 1)
     residual = lax.dynamic_slice_in_dim(all_rows, offset, half_cols, 1).astype(jnp.float32)
     gain_part = lax.dynamic_slice_in_dim(post_gain, offset, half_cols, 0)

time: 139 us -> 130 us (0.935)
  waiting for transfers between devices: 47.9 us -> 39 us
  other arithmetic: 24.3 us -> 26 us
  local copies, waits for them, and re-layouts: 19.8 us -> 18.3 us
    psum x1 -> x0, waiting for transfers between devices: 20.9 us -> none  [on_device(): summed = lax.psum(partial_rows, 'head')]
    all_gather x0 -> x1, waiting for transfers between devices: none -> 11.8 us  [on_device(): summed = jnp.sum(lax.all_gather(partial_rows, 'head'), axis=0)]
    reduce_sum x0 -> x1, other arithmetic: none -> 4.2 us  [on_device(): summed = jnp.sum(lax.all_gather(partial_rows, 'head'), axis=0)]
    another operation x1, other arithmetic: 1.66 us -> 0.07 us  [on_device(): jnp.stack([key_rows, value_rows], axis=2).reshape(all_rows.shape[0], -1)]
  transfers between devices with their start and end apart: 2 -> 2, of which waited for: 2 -> 2; matrix products, arithmetic and copies ran while one was open for 21% -> 19% of each run, Pallas kernels for 0% -> 0%
where the time goes in v1:
time: 130 us
  waiting for transfers between devices  39 us (30%)
  other arithmetic  26 us (20%)
  local copies, waits for them, and re-layouts  18.3 us (14%)
  starting transfers between devices  17.2 us (13%)
  between operations  15.7 us (12%)
  matrix products  13.3 us (10%)
    all_to_all x1, waiting for transfers between devices, on_device(): lax.all_to_all(outgoing, 'req', split_axis=0, concat_axis=0, tiled=True)  27.2 us
    all_to_all x1, starting transfers between devices, on_device(): lax.all_to_all(outgoing, 'req', split_axis=0, concat_axis=0, tiled=True)  17 us
    all_gather x1, waiting for transfers between devices, on_device(): summed = jnp.sum(lax.all_gather(partial_rows, 'head'), axis=0)  11.8 us
    dot_general x1, matrix products, on_device(): partial_rows = jnp.dot(all_attn, w_out, preferred_element_type=jnp.float32)  4.93 us
    reduce_sum x5, other arithmetic, rms_scale(): jnp.mean(values * values, axis=-1, keepdims=True) + eps_norm  4.76 us
    dot_general x1, matrix products, project(): jnp.dot(normed, w_query, preferred_element_type=jnp.float32)  4.6 us
    reduce_sum x1, other arithmetic, on_device(): summed = jnp.sum(lax.all_gather(partial_rows, 'head'), axis=0)  4.2 us
    gather x2, local copies, waits for them, and re-layouts, verify_one(): cached = jnp.take(pool_now, page_list, axis=0).reshape(-1, groups, 2, HEAD)  3.76 us
  transfers between devices with their start and end apart: 2, of which 2 were waited for; matrix products, arithmetic and copies ran while one was open for 19% of the time, Pallas kernels for 0%

profile of v1, /device:TPU:1, one launch (start us, length us, event | category | flops | bytes accessed | tf_op | source)
XLA Modules:
  0.0 129.5 jit_solution(15474953056323952004)
XLA Ops:
  9.3 3.3 %gather_fusion = bf16[128,16,512]{2,1,0:T(8,128)(2,1)} fusion(bf16[64,16,512]{2,1,0:T(8,128)(2,1)} %param.22, s32[1024]{0:T(1024)S(1)} %pad_clamp_fusion.1), kind=kCustom, calls=%fused_computation | custom fusion | bytes 4194816 | tf_op jit(solution)/shard_map/jit(_take)/gather | solution.py:91
  12.6 3.0 %select_select_fusion = bf16[128,16,512]{2,1,0:T(8,128)(2,1)} fusion(bf16[128,16,512]{2,1,0:T(8,128)(2,1)} %gather_fusion, pred[128]{0:T(512)(128)(4,1)S(1)} %compare_and_fusion, pred[128]{0:T(512)(128)(4,1)S(1)} %compare_bitcast_fusion), kind=kLoop, calls=%fused_computation.12 | loop fusion | flops 2097152 | bytes 4194560 | tf_op jit(solution)/shard_map/jit(_where)/select_n | solution.py:92
  15.6 17.0 %all-to-all-start = ((bf16[128,16,512]{2,1,0:T(8,128)(2,1)}), bf16[128,16,512]{2,1,0:T(8,128)(2,1)}, u32[]{:S(2)}, u32[]{:S(2)}) async-start(bf16[128,16,512]{2,1,0:T(8,128)(2,1)} %select_select_fusion), calls=%async_computation | async-start | bytes 4194304 | tf_op jit(solution)/shard_map/all_to_all | solution.py:93
  36.9 1.6 %fusion.50 = f32[261,512]{1,0:T(8,128)} fusion(bf16[2048,512]{1,0:T(8,128)(2,1)S(1)} %copy-done, f32[2048]{0:T(1024)S(1)} %copy-done.17, f32[261]{0:T(512)S(1)} %add_rsqrt_fusion.4, bf16[256,2048]{1,0:T(8,128)(2,1)S(1)} %copy-done.3, bf16[5,2048]{1,0:T(8,128)(2,1)S(1)} %bitcast.117), kind=kOutput, calls=%fused_computation.125 | convolution fusion | flops 551098368 | bytes 3709972 | tf_op jit(solution)/shard_map/dot_general | solution.py:36
  38.5 2.2 %reshape.682 = f32[261,1,2,256]{3,2,0,1:T(2,128)} reshape(f32[261,512]{1,0:T(8,128)} %fusion.50) | data formatting | bytes 1069056 | tf_op jit(solution)/shard_map/reshape | solution.py:36
  40.7 1.7 %fusion.52 = (f32[261,1,1,256]{3,2,0,1:T(1,128)S(1)}, f32[261,1,1,256]{3,2,0,1:T(1,128)S(1)}) fusion(f32[261,1,2,256]{3,2,0,1:T(2,128)} %reshape.682), kind=kLoop, calls=%fused_computation.126 | loop fusion | bytes 1069056 | tf_op jit(solution)/shard_map/slice | solution.py:40
  43.2 4.6 %fusion.48 = f32[261,1024]{1,0:T(8,128)} fusion(bf16[2048,1024]{1,0:T(8,128)(2,1)} %param.17, f32[2048]{0:T(1024)S(1)} %copy-done.17, f32[261]{0:T(512)S(1)} %add_rsqrt_fusion.4, bf16[256,2048]{1,0:T(8,128)(2,1)S(1)} %copy-done.3, bf16[5,2048]{1,0:T(8,128)(2,1)S(1)} %bitcast.118), kind=kOutput, calls=%fused_computation.124 | convolution fusion | flops 1098455040 | bytes 6341652 | tf_op jit(solution)/shard_map/dot_general | solution.py:32
  47.8 1.8 %reshape.689 = f32[261,4,256]{2,1,0:T(4,128)S(1)} reshape(f32[261,1024]{1,0:T(8,128)} %fusion.48) | data formatting | bytes 2138112 | tf_op jit(solution)/shard_map/reshape | solution.py:32
  49.6 1.0 multiply_reduce_fusion.1
  50.6 1.0 copy.55
  51.7 1.1 fusion.20
  52.8 1.2 fusion.28
  54.2 1.1 multiply_cosine_fusion
  56.5 1.2 convolution_convert_fusion
  57.7 27.2 %all-to-all-done = bf16[128,16,512]{2,1,0:T(8,128)(2,1)} async-done(((bf16[128,16,512]{2,1,0:T(8,128)(2,1)}), bf16[128,16,512]{2,1,0:T(8,128)(2,1)}, u32[]{:S(2)}, u32[]{:S(2)}) %all-to-all-start) | async-done | bytes 2097184 | tf_op jit(solution)/shard_map/all_to_all | solution.py:93
  84.9 3.5 %pad_maximum_fusion = bf16[192,16,512]{2,1,0:T(8,128)(2,1)} fusion(bf16[128,16,512]{2,1,0:T(8,128)(2,1)} %all-to-all-done, bf16[64,16,512]{2,1,0:T(8,128)(2,1)S(1)} %copy-done.2), kind=kLoop, calls=%fused_computation.2 | loop fusion | flops 1572864 | bytes 6291456 | tf_op jit(solution)/shard_map/concatenate | solution.py:94
  88.5 2.6 %gather_fusion.1 = bf16[64,16,512]{2,1,0:T(8,128)(2,1)S(1)} fusion(bf16[192,16,512]{2,1,0:T(8,128)(2,1)} %pad_maximum_fusion, s32[1024]{0:T(1024)} %pad_clamp_fusion), kind=kCustom, calls=%fused_computation.1 | custom fusion | bytes 2097408 | tf_op jit(solution)/shard_map/vmap(jit(_take))/gather | solution.py:110
  91.1 1.1 gather.12
  92.2 1.5 %copy_select_fusion = bf16[1,1024,1,2,256]{4,1,3,2,0:T(8,128)(2,1)S(1)} fusion(bf16[1,1024,1,2,256]{4,3,1,2,0:T(2,128)(2,1)} %gather.12, pred[1024]{0:T(1024)(128)(4,1)S(1)} %copy-done.15), kind=kLoop, calls=%fused_computation.26 | loop fusion | flops 524288 | bytes 2098176 | tf_op jit(solution)/shard_map/vmap(jit(_take))/select_n | solution.py:110
  94.8 4.9 %convolution_bitcast_fusion = f32[1,261,2048]{2,1,0:T(8,128)} fusion(bf16[1024,2048]{1,0:T(8,128)(2,1)} %param.20, bf16[256,1024]{0,1:T(8,128)(2,1)S(1)} %bitcast.125, bf16[5,1024]{0,1:T(8,128)(2,1)S(1)} %copy.59), kind=kOutput, calls=%fused_computation.3 | convolution fusion | flops 1095782400 | bytes 6866944 | tf_op jit(solution)/shard_map/dot_general | solution.py:137
  102.4 11.8 %all-gather.4.cloned.1.call-done = f32[2,261,2048]{2,1,0:T(8,128)} async-done(((f32[1,261,2048]{2,1,0:T(8,128)}), f32[2,261,2048]{2,1,0:T(8,128)}) %all-gather.4.cloned.1.call-update) | async-done | bytes 4276240 | tf_op jit(solution)/shard_map/all_gather | solution.py:140
  114.2 4.2 %reduce_sum.98 = f32[261,2048]{1,0:T(8,128)} reduce(f32[2,261,2048]{2,1,0:T(8,128)} %all-gather.4.cloned.1.call-done, f32[]{:T(128)} %constant.39.clone.1), dimensions={0}, to_apply=%region_11.12 | reduce | flops 534528 | bytes 6414340 | tf_op jit(solution)/shard_map/reduce_sum | solution.py:140
  118.4 2.0 %multiply_reduce_fusion = f32[261]{0:T(512)S(1)} fusion(f32[261,2048]{1,0:T(8,128)} %reduce_sum.98), kind=kLoop, calls=%fused_computation.11 | loop fusion | flops 1068795 | bytes 2139156 | tf_op jit(solution)/shard_map/reduce_sum | solution.py:13
  121.7 0.9 slice.103
  (96 shorter events, 12.2 us)
Async XLA Ops:
  7.2 29.7 %copy-start = (bf16[2048,512]{1,0:T(8,128)(2,1)S(1)}, bf16[2048,512]{1,0:T(8,128)(2,1)}, u32[]{:S(2)}) copy-start(bf16[2048,512]{1,0:T(8,128)(2,1)} %param.18) | copy-start | bytes 6291460
  15.6 17.8 %copy-start.18 = (s32[1,64]{1,0:T(1,128)S(1)}, s32[1,64]{1,0:T(1,128)}, u32[]{:S(2)}) copy-start(s32[1,64]{1,0:T(1,128)} %param.24) | copy-start | bytes 772
  15.6 18.5 %copy-start.19 = (s32[1,4]{1,0:T(1,128)S(1)}, s32[1,4]{1,0:T(1,128)}, u32[]{:S(2)}) copy-start(s32[1,4]{1,0:T(1,128)} %param.26) | copy-start | bytes 52
  15.6 18.8 %copy-start.3 = (bf16[256,2048]{1,0:T(8,128)(2,1)S(1)}, bf16[256,2048]{1,0:T(8,128)(2,1)}, u32[]{:S(2)}) copy-start(bf16[256,2048]{1,0:T(8,128)(2,1)} %param.15) | copy-start | bytes 3145732
  15.6 18.8 %copy-start.12 = (bf16[1,5,2048]{2,1,0:T(8,128)(2,1)S(1)}, bf16[1,5,2048]{2,1,0:T(8,128)(2,1)}, u32[]{:S(2)}) copy-start(bf16[1,5,2048]{2,1,0:T(8,128)(2,1)} %param.14) | copy-start | bytes 61444
  15.6 21.3 %copy-start.17 = (f32[2048]{0:T(1024)S(1)}, f32[2048]{0:T(1024)}, u32[]{:S(2)}) copy-start(f32[2048]{0:T(1024)} %param.16) | copy-start | bytes 24580
  15.6 69.3 %all-to-all-start = ((bf16[128,16,512]{2,1,0:T(8,128)(2,1)}), bf16[128,16,512]{2,1,0:T(8,128)(2,1)}, u32[]{:S(2)}, u32[]{:S(2)}) async-start(bf16[128,16,512]{2,1,0:T(8,128)(2,1)} %select_select_fusion), calls=%async_computation | async-start | bytes 4194304 | tf_op jit(solution)/shard_map/all_to_all | solution.py:93
  32.6 81.6 %all-gather.4.cloned.1.call-start = ((), (), s32[]{:S(2)}) async-start(), calls=%async_computation.1 | async-start | bytes 6488064 | tf_op jit(solution)/shard_map/all_gather | solution.py:140
  42.3 0.7 copy-start.5
  47.8 3.9 %copy-start.16 = (f32[2,256]{1,0:T(2,128)S(1)}, f32[2,256]{1,0:T(2,128)}, u32[]{:S(2)}) copy-start(f32[2,256]{1,0:T(2,128)} %param.19) | copy-start | bytes 6148
  54.0 1.7 %copy-start.6 = (bf16[261,1,128]{2,0,1:T(8,128)(2,1)}, bf16[261,1,128]{2,0,1:T(8,128)(2,1)S(1)}, u32[]{:S(2)}) copy-start(bf16[261,1,128]{2,0,1:T(8,128)(2,1)S(1)} %get-tuple-element.27) | copy-start | bytes 200452
  55.7 1.9 %copy-start.8 = (bf16[261,4,128]{2,0,1:T(8,128)(2,1)}, bf16[261,4,128]{2,0,1:T(8,128)(2,1)S(1)}, u32[]{:S(2)}) copy-start(bf16[261,4,128]{2,0,1:T(8,128)(2,1)S(1)} %get-tuple-element.20) | copy-start | bytes 801796
  55.7 1.9 %copy-start.10 = (bf16[261,4,128]{2,0,1:T(8,128)(2,1)}, bf16[261,4,128]{2,0,1:T(8,128)(2,1)S(1)}, u32[]{:S(2)}) copy-start(bf16[261,4,128]{2,0,1:T(8,128)(2,1)S(1)} %get-tuple-element.21) | copy-start | bytes 801796
  56.4 1.2 copy-start.13
  56.4 1.2 copy-start.14
  56.4 28.5 %copy-start.2 = (bf16[64,16,512]{2,1,0:T(8,128)(2,1)S(1)}, bf16[64,16,512]{2,1,0:T(8,128)(2,1)}, u32[]{:S(2)}) copy-start(bf16[64,16,512]{2,1,0:T(8,128)(2,1)} %param.22) | copy-start | bytes 3145732
  88.5 3.8 %copy-start.15 = (pred[1024]{0:T(1024)(128)(4,1)S(1)}, pred[1024]{0:T(1024)(128)(4,1)}, u32[]{:S(2)}) copy-start(pred[1024]{0:T(1024)(128)(4,1)} %broadcast_in_dim.141) | copy-start | bytes 3076
  92.2 1.6 %copy-start.9 = (bf16[261,4,128]{2,0,1:T(8,128)(2,1)S(1)}, bf16[261,4,128]{2,0,1:T(8,128)(2,1)}, u32[]{:S(2)}) copy-start(bf16[261,4,128]{2,0,1:T(8,128)(2,1)} %copy-done.8) | copy-start | bytes 801796
  92.2 1.6 %copy-start.11 = (bf16[261,4,128]{2,0,1:T(8,128)(2,1)S(1)}, bf16[261,4,128]{2,0,1:T(8,128)(2,1)}, u32[]{:S(2)}) copy-start(bf16[261,4,128]{2,0,1:T(8,128)(2,1)} %copy-done.10) | copy-start | bytes 801796
  93.8 1.0 copy-start.20
  99.8 0.9 copy-start.7
  114.2 6.2 %copy-start.4 = (bf16[256,2048]{1,0:T(8,128)(2,1)S(1)}, bf16[256,2048]{1,0:T(8,128)(2,1)}, u32[]{:S(2)}) copy-start(bf16[256,2048]{1,0:T(8,128)(2,1)} %param.15) | copy-start | bytes 3145732
  118.4 2.3 %copy-start.1 = (f32[261,2048]{1,0:T(8,128)S(1)}, f32[261,2048]{1,0:T(8,128)}, u32[]{:S(2)}) copy-start(f32[261,2048]{1,0:T(8,128)} %reduce_sum.98) | copy-start | bytes 6414340
  118.4 2.3 %dynamic-slice-start = ((f32[2048]{0:T(1024)}, s32[]{:T(128)}), f32[1024]{0:T(1024)S(1)}, s32[]{:S(2)}) async-start(f32[2048]{0:T(1024)} %param.21, s32[]{:T(128)} %select_n.81), calls=%async_computation.2 | async-start | bytes 8704 | tf_op jit(solution)/shard_map/dynamic_slice | solution.py:143
Sparse Core Ops, SparseCore 0:
  99.9 14.2 all-gather.3
